TPU v7x, 32 devices: a whole 2x2x4 slice. The times are simulated.
32 devices in a mesh: dp: 4 (over y, x), seq: 8 (over z, core).
Axes of the slice: x: 2, y: 2, z: 4, core: 2. Of those that a mesh axis runs over, the one named last changes fastest.
Arguments:
- hidden_in: bfloat16 [8, 1024, 1536], P('dp', 'seq'), may hold values from -6 to 6
- lengths: int32 [8], P('dp'), may hold values from 256 to 1024, as said below
- cotangent: bfloat16 [8, 1024, 1536], P('dp', 'seq'), may hold values from -6 to 6
- attn_gain: bfloat16 [1536], P(('dp', 'seq')), may hold values from 0.25 to 1.75
- q_weight: bfloat16 [1536, 1536], P(('dp', 'seq')), may hold values from -0.15625 to 0.15625
- q_bias: bfloat16 [1536], P(('dp', 'seq')), may hold values from -3 to 3
- k_weight: bfloat16 [256, 1536], P(('dp', 'seq')), may hold values from -0.15625 to 0.15625
- k_bias: bfloat16 [256], P(('dp', 'seq')), may hold values from -3 to 3
- v_weight: bfloat16 [256, 1536], P(('dp', 'seq')), may hold values from -0.15625 to 0.15625
- v_bias: bfloat16 [256], P(('dp', 'seq')), may hold values from -0.59765625 to 0.59765625
- o_weight: bfloat16 [1536, 1536], P(('dp', 'seq')), may hold values from -0.875 to 0.875
- mlp_gain: bfloat16 [1536], P(('dp', 'seq')), may hold values from 0.25 to 1.75
- gate_weight: bfloat16 [8960, 1536], P(('dp', 'seq')), may hold values from -0.15625 to 0.15625
- up_weight: bfloat16 [8960, 1536], P(('dp', 'seq')), may hold values from -0.15625 to 0.15625
- down_weight: bfloat16 [1536, 8960], P(None, ('dp', 'seq')), may hold values from -0.0625 to 0.0625
Outputs:
- block_out: bfloat16 [8, 1024, 1536], P('dp', 'seq')
- input_grad: float32 [8, 1024, 1536], P('dp', 'seq')
- attn_gain_grad: float32 [1536], P(('dp', 'seq'))
- q_weight_grad: float32 [1536, 1536], P(('dp', 'seq'))
- q_bias_grad: float32 [1536], P(('dp', 'seq'))
- k_weight_grad: float32 [256, 1536], P(('dp', 'seq'))
- k_bias_grad: float32 [256], P(('dp', 'seq'))
- v_weight_grad: float32 [256, 1536], P(('dp', 'seq'))
- v_bias_grad: float32 [256], P(('dp', 'seq'))
- o_weight_grad: float32 [1536, 1536], P(('dp', 'seq'))
- mlp_gain_grad: float32 [1536], P(('dp', 'seq'))
- gate_weight_grad: float32 [8960, 1536], P(('dp', 'seq'))
- up_weight_grad: float32 [8960, 1536], P(('dp', 'seq'))
- down_weight_grad: float32 [1536, 8960], P(None, ('dp', 'seq'))
Inputs may be any that keep to these rules, and one draw needn't show every extreme that they name: Slots t < lengths[b] of sequence b are valid; in every draw at least one sequence is valid in all 1024 slots.
All inputs are finite; a program needn't handle non-finite values.
Results may differ from a plain program's by a relative error of at most 0.025.
Values may be sent and summed in bfloat16 or wider, within the bound.
No kernel may reach another device: no remote copies, remote signals or barrier semaphores. Data moves between devices by JAX's collectives and lax.ppermute only.
A program may use at most 448 MiB of HBM per device.

v0:
```python
import math

import jax
import jax.numpy as jnp
from jax import lax
from jax.sharding import PartitionSpec as P

HEADS = 12
KV_HEADS = 2
HEAD = 128


EPSILON = 1e-06
NEGATIVE = -1e30


def times_transposed(left_side, right_side):
    return lax.dot_general(
        left_side, right_side, (((1,), (1,)), ((), ())), preferred_element_type=jnp.float32
    )


def plain_product(left_side, right_side):
    return jnp.dot(left_side, right_side, preferred_element_type=jnp.float32)


def split_columns(values, group_count):
    row_count, width = values.shape
    return values.reshape(row_count, group_count, width // group_count)


def owner_grad(columns, inputs_all):
    part_grad = jnp.einsum("rpf,rd->pfd", columns, inputs_all, preferred_element_type=jnp.float32)
    return part_grad.reshape(-1, inputs_all.shape[1])


def owner_bias(columns):
    return jnp.sum(columns.astype(jnp.float32), axis=0).reshape(-1)


def rope_tables(positions):
    half_size = HEAD // 2
    inverse = jnp.exp(-math.log(1000000.0) * 2.0 * jnp.arange(half_size).astype(jnp.float32) / HEAD)
    angles = positions[:, None] * inverse[None, :]
    angles = jnp.concatenate([angles, angles], axis=1)
    return (jnp.cos(angles), jnp.sin(angles))


def rotate(values, cosine, sine_table):
    half_size = HEAD // 2
    turned = jnp.concatenate([-values[..., half_size:], values[..., :half_size]], axis=-1)
    return values * cosine[:, None, :] + turned * sine_table[:, None, :]


def rotate_back(gradient, cosine, sine_table):
    half_size = HEAD // 2
    scaled = gradient * sine_table[:, None, :]
    turned = jnp.concatenate([scaled[..., half_size:], -scaled[..., :half_size]], axis=-1)
    return gradient * cosine[:, None, :] + turned


def rms_parts(values):
    inverse = lax.rsqrt(jnp.mean(values * values, axis=-1, keepdims=True) + EPSILON)
    return (values * inverse, inverse)


def rms_back(upstream, normal_values, inverse, gain_values):
    scaled = upstream * gain_values
    gain_grad = jnp.sum(upstream * normal_values, axis=0)
    input_part = inverse * (
        scaled - normal_values * jnp.mean(scaled * normal_values, axis=-1, keepdims=True)
    )
    return (input_part, gain_grad)


def masked_scores(query_heads, key_heads, causal, score_scale):
    scores = (
        jnp.einsum("qkgd,skd->kgqs", query_heads, key_heads, preferred_element_type=jnp.float32)
        * score_scale
    )
    return jnp.where(causal[None, None], scores, NEGATIVE)


def on_device(
    hidden_in,
    lengths,
    cotangent,
    attn_gain,
    q_weight,
    q_bias,
    k_weight,
    k_bias,
    v_weight,
    v_bias,
    o_weight,
    mlp_gain,
    gate_weight,
    up_weight,
    down_weight,
):
    micro_count, span_rows, model_width = hidden_in.shape
    rows = micro_count * span_rows
    full_len = span_rows * lax.axis_size("seq")
    dp_count = lax.axis_size("dp")
    group_share = HEADS // KV_HEADS
    kv_width = KV_HEADS * HEAD
    score_scale = 1.0 / math.sqrt(HEAD)
    positions = lax.axis_index("seq") * span_rows + jnp.arange(span_rows, dtype=jnp.int32)
    cosine, sine_table = rope_tables(positions.astype(jnp.float32))
    causal = positions[:, None] >= jnp.arange(full_len, dtype=jnp.int32)[None, :]
    gathered = (
        lax.all_gather(attn_gain, ("dp", "seq"), axis=0, tiled=True),
        lax.all_gather(q_weight, ("dp", "seq"), axis=0, tiled=True),
        lax.all_gather(q_bias, ("dp", "seq"), axis=0, tiled=True),
        lax.all_gather(k_weight, ("dp", "seq"), axis=0, tiled=True),
        lax.all_gather(k_bias, ("dp", "seq"), axis=0, tiled=True),
        lax.all_gather(v_weight, ("dp", "seq"), axis=0, tiled=True),
        lax.all_gather(v_bias, ("dp", "seq"), axis=0, tiled=True),
        lax.all_gather(o_weight, ("dp", "seq"), axis=0, tiled=True),
        lax.all_gather(mlp_gain, ("dp", "seq"), axis=0, tiled=True),
    )
    gain_one, query_w, query_b, key_w, key_b, value_w, value_b, output_w, gain_two = gathered
    inputs = hidden_in.reshape(rows, model_width).astype(jnp.float32)
    normal_one, inverse_one = rms_parts(inputs)
    attn_in = (normal_one * gain_one.astype(jnp.float32)).astype(jnp.bfloat16)
    query_lin = times_transposed(attn_in, query_w) + query_b.astype(jnp.float32)
    key_lin = times_transposed(attn_in, key_w) + key_b.astype(jnp.float32)
    value_lin = times_transposed(attn_in, value_w) + value_b.astype(jnp.float32)
    query_rot = rotate(
        query_lin.reshape(micro_count, span_rows, HEADS, HEAD), cosine, sine_table
    ).astype(jnp.bfloat16)
    key_rot = (
        rotate(key_lin.reshape(micro_count, span_rows, KV_HEADS, HEAD), cosine, sine_table)
        .astype(jnp.bfloat16)
        .reshape(micro_count, span_rows, kv_width)
    )
    value_low = value_lin.astype(jnp.bfloat16).reshape(micro_count, span_rows, kv_width)
    key_all, value_all = (
        lax.all_gather(key_rot, "seq", axis=1, tiled=True),
        lax.all_gather(value_low, "seq", axis=1, tiled=True),
    )
    query_heads = query_rot.reshape(micro_count, span_rows, KV_HEADS, group_share, HEAD)
    key_heads = key_all.reshape(micro_count, full_len, KV_HEADS, HEAD)
    value_heads = value_all.reshape(micro_count, full_len, KV_HEADS, HEAD)
    mixed_parts = []
    log_parts = []
    for batch_index in range(micro_count):
        scores = masked_scores(
            query_heads[batch_index], key_heads[batch_index], causal, score_scale
        )
        row_top = jnp.max(scores, axis=-1, keepdims=True)
        exponent = jnp.exp(scores - row_top)
        row_total = jnp.sum(exponent, axis=-1, keepdims=True)
        log_parts.append(row_top + jnp.log(row_total))
        soft_low = (exponent / row_total).astype(jnp.bfloat16)
        mixed_heads = jnp.einsum(
            "kgqs,skd->qkgd", soft_low, value_heads[batch_index], preferred_element_type=jnp.float32
        )
        mixed_parts.append(mixed_heads.reshape(span_rows, model_width))
    mixed_low = jnp.concatenate(mixed_parts, axis=0).astype(jnp.bfloat16)
    resid = inputs + times_transposed(mixed_low, output_w)
    normal_two, inverse_two = rms_parts(resid)
    mlp_in = (normal_two * gain_two.astype(jnp.float32)).astype(jnp.bfloat16)
    gate_w, up_w, down_w = (
        lax.all_gather(gate_weight, ("dp", "seq"), axis=0, tiled=True),
        lax.all_gather(up_weight, ("dp", "seq"), axis=0, tiled=True),
        lax.all_gather(down_weight, ("dp", "seq"), axis=1, tiled=True),
    )
    gate_lin = times_transposed(mlp_in, gate_w)
    up_lin = times_transposed(mlp_in, up_w)
    gate_sigma = jax.nn.sigmoid(gate_lin)
    hidden_low = (gate_lin * gate_sigma * up_lin).astype(jnp.bfloat16)
    result = resid + times_transposed(hidden_low, down_w)
    valid_rows = (positions[None, :] < lengths[:, None]).reshape(rows)
    block_out = (
        jnp.where(valid_rows[:, None], result, 0.0)
        .astype(jnp.bfloat16)
        .reshape(micro_count, span_rows, model_width)
    )
    back_query, back_key, back_value, back_output, back_gate, back_up, back_down = (
        lax.all_gather(q_weight, ("dp", "seq"), axis=0, tiled=True),
        lax.all_gather(k_weight, ("dp", "seq"), axis=0, tiled=True),
        lax.all_gather(v_weight, ("dp", "seq"), axis=0, tiled=True),
        lax.all_gather(o_weight, ("dp", "seq"), axis=0, tiled=True),
        lax.all_gather(gate_weight, ("dp", "seq"), axis=0, tiled=True),
        lax.all_gather(up_weight, ("dp", "seq"), axis=0, tiled=True),
        lax.all_gather(down_weight, ("dp", "seq"), axis=1, tiled=True),
    )
    upstream = jnp.where(
        valid_rows[:, None], cotangent.reshape(rows, model_width).astype(jnp.float32), 0.0
    )
    upstream_low = upstream.astype(jnp.bfloat16)
    attn_all, mixed_all, mlp_all, upstream_all = (
        lax.all_gather(attn_in, "seq", axis=0, tiled=True),
        lax.all_gather(mixed_low, "seq", axis=0, tiled=True),
        lax.all_gather(mlp_in, "seq", axis=0, tiled=True),
        lax.all_gather(upstream_low, "seq", axis=0, tiled=True),
    )
    hidden_grad = plain_product(upstream_low, back_down)
    gate_grad = (
        hidden_grad * up_lin * (gate_sigma * (1.0 + gate_lin * (1.0 - gate_sigma)))
    ).astype(jnp.bfloat16)
    up_grad = (hidden_grad * gate_lin * gate_sigma).astype(jnp.bfloat16)
    mlp_in_grad = plain_product(gate_grad, back_gate) + plain_product(up_grad, back_up)
    hidden_cols, gate_cols, up_cols = (
        lax.all_to_all(
            split_columns(hidden_low, dp_count), "seq", split_axis=2, concat_axis=0, tiled=True
        ),
        lax.all_to_all(
            split_columns(gate_grad, dp_count), "seq", split_axis=2, concat_axis=0, tiled=True
        ),
        lax.all_to_all(
            split_columns(up_grad, dp_count), "seq", split_axis=2, concat_axis=0, tiled=True
        ),
    )
    down_grad = jnp.einsum(
        "rd,rpf->dpf", upstream_all, hidden_cols, preferred_element_type=jnp.float32
    ).reshape(model_width, -1)
    gate_w_grad = owner_grad(gate_cols, mlp_all)
    up_w_grad = owner_grad(up_cols, mlp_all)
    norm_two_grad, gain_two_grad = rms_back(
        mlp_in_grad, normal_two, inverse_two, gain_two.astype(jnp.float32)
    )
    resid_grad = upstream + norm_two_grad
    resid_low = resid_grad.astype(jnp.bfloat16)
    mixed_grad = (
        plain_product(resid_low, back_output)
        .astype(jnp.bfloat16)
        .reshape(micro_count, span_rows, KV_HEADS, group_share, HEAD)
    )
    query_parts = []
    key_parts = []
    value_parts = []
    for batch_index in range(micro_count):
        again_scores = masked_scores(
            query_heads[batch_index], key_heads[batch_index], causal, score_scale
        )
        soft_probs = jnp.exp(again_scores - log_parts[batch_index])
        probs_low = soft_probs.astype(jnp.bfloat16)
        prob_grad = jnp.einsum(
            "qkgd,skd->kgqs",
            mixed_grad[batch_index],
            value_heads[batch_index],
            preferred_element_type=jnp.float32,
        )
        value_all_grad = jnp.einsum(
            "kgqs,qkgd->skd", probs_low, mixed_grad[batch_index], preferred_element_type=jnp.float32
        )
        row_delta = jnp.sum(soft_probs * prob_grad, axis=-1, keepdims=True)
        score_grad = (soft_probs * (prob_grad - row_delta)).astype(jnp.bfloat16)
        query_parts.append(
            jnp.einsum(
                "kgqs,skd->qkgd",
                score_grad,
                key_heads[batch_index],
                preferred_element_type=jnp.float32,
            )
            * score_scale
        )
        key_parts.append(
            (
                jnp.einsum(
                    "kgqs,qkgd->skd",
                    score_grad,
                    query_heads[batch_index],
                    preferred_element_type=jnp.float32,
                )
                * score_scale
            ).reshape(full_len, kv_width)
        )
        value_parts.append(value_all_grad.reshape(full_len, kv_width))
    key_grad, value_grad = (
        lax.psum_scatter(jnp.stack(key_parts), "seq", scatter_dimension=1, tiled=True),
        lax.psum_scatter(jnp.stack(value_parts), "seq", scatter_dimension=1, tiled=True),
    )
    query_grad = jnp.stack(query_parts).reshape(micro_count, span_rows, HEADS, HEAD)
    query_low = (
        rotate_back(query_grad, cosine, sine_table).reshape(rows, model_width).astype(jnp.bfloat16)
    )
    key_low = (
        rotate_back(key_grad.reshape(micro_count, span_rows, KV_HEADS, HEAD), cosine, sine_table)
        .reshape(rows, kv_width)
        .astype(jnp.bfloat16)
    )
    value_grad_low = value_grad.reshape(rows, kv_width).astype(jnp.bfloat16)
    attn_in_grad = (
        plain_product(query_low, back_query)
        + plain_product(key_low, back_key)
        + plain_product(value_grad_low, back_value)
    )
    norm_one_grad, gain_one_grad = rms_back(
        attn_in_grad, normal_one, inverse_one, gain_one.astype(jnp.float32)
    )
    input_grad = (resid_grad + norm_one_grad).reshape(micro_count, span_rows, model_width)
    resid_cols, query_cols, key_cols, value_cols = (
        lax.all_to_all(
            split_columns(resid_low, dp_count), "seq", split_axis=2, concat_axis=0, tiled=True
        ),
        lax.all_to_all(
            split_columns(query_low, dp_count), "seq", split_axis=2, concat_axis=0, tiled=True
        ),
        lax.all_to_all(
            split_columns(key_low, dp_count), "seq", split_axis=2, concat_axis=0, tiled=True
        ),
        lax.all_to_all(
            split_columns(value_grad_low, dp_count), "seq", split_axis=2, concat_axis=0, tiled=True
        ),
    )
    output_w_grad = owner_grad(resid_cols, mixed_all)
    query_w_grad = owner_grad(query_cols, attn_all)
    key_w_grad = owner_grad(key_cols, attn_all)
    value_w_grad = owner_grad(value_cols, attn_all)
    query_b_grad = owner_bias(query_cols)
    key_b_grad = owner_bias(key_cols)
    value_b_grad = owner_bias(value_cols)
    totals = (
        lax.psum_scatter(
            query_w_grad.astype(jnp.bfloat16), "dp", scatter_dimension=0, tiled=True
        ).astype(jnp.float32),
        lax.psum_scatter(
            query_b_grad.astype(jnp.bfloat16), "dp", scatter_dimension=0, tiled=True
        ).astype(jnp.float32),
        lax.psum_scatter(
            key_w_grad.astype(jnp.bfloat16), "dp", scatter_dimension=0, tiled=True
        ).astype(jnp.float32),
        lax.psum_scatter(
            key_b_grad.astype(jnp.bfloat16), "dp", scatter_dimension=0, tiled=True
        ).astype(jnp.float32),
        lax.psum_scatter(
            value_w_grad.astype(jnp.bfloat16), "dp", scatter_dimension=0, tiled=True
        ).astype(jnp.float32),
        lax.psum_scatter(
            value_b_grad.astype(jnp.bfloat16), "dp", scatter_dimension=0, tiled=True
        ).astype(jnp.float32),
        lax.psum_scatter(
            output_w_grad.astype(jnp.bfloat16), "dp", scatter_dimension=0, tiled=True
        ).astype(jnp.float32),
        lax.psum_scatter(
            gate_w_grad.astype(jnp.bfloat16), "dp", scatter_dimension=0, tiled=True
        ).astype(jnp.float32),
        lax.psum_scatter(
            up_w_grad.astype(jnp.bfloat16), "dp", scatter_dimension=0, tiled=True
        ).astype(jnp.float32),
        lax.psum_scatter(
            down_grad.astype(jnp.bfloat16), "dp", scatter_dimension=1, tiled=True
        ).astype(jnp.float32),
    )
    gain_totals = (
        lax.psum_scatter(gain_one_grad, ("dp", "seq"), scatter_dimension=0, tiled=True),
        lax.psum_scatter(gain_two_grad, ("dp", "seq"), scatter_dimension=0, tiled=True),
    )
    return (
        block_out,
        input_grad,
        gain_totals[0],
        totals[0],
        totals[1],
        totals[2],
        totals[3],
        totals[4],
        totals[5],
        totals[6],
        gain_totals[1],
        totals[7],
        totals[8],
        totals[9],
    )


def solution(mesh):
    placed = (
        P("dp", "seq", None),
        P("dp"),
        P("dp", "seq", None),
        P(("dp", "seq")),
        P(("dp", "seq"), None),
        P(("dp", "seq")),
        P(("dp", "seq"), None),
        P(("dp", "seq")),
        P(("dp", "seq"), None),
        P(("dp", "seq")),
        P(("dp", "seq"), None),
        P(("dp", "seq")),
        P(("dp", "seq"), None),
        P(("dp", "seq"), None),
        P(None, ("dp", "seq")),
    )
    return jax.shard_map(
        on_device,
        mesh=mesh,
        in_specs=placed,
        out_specs=(
            P("dp", "seq", None),
            P("dp", "seq", None),
            P(("dp", "seq")),
            P(("dp", "seq"), None),
            P(("dp", "seq")),
            P(("dp", "seq"), None),
            P(("dp", "seq")),
            P(("dp", "seq"), None),
            P(("dp", "seq")),
            P(("dp", "seq"), None),
            P(("dp", "seq")),
            P(("dp", "seq"), None),
            P(("dp", "seq"), None),
            P(None, ("dp", "seq")),
        ),
        check_vma=False,
    )
```

profile of v0, /device:TPU:0, one launch (start us, length us, event | category | flops | bytes accessed | tf_op | source)
XLA Modules:
  0.0 1691.2 jit_solution(5494307519598988704)
XLA Ops:
  11.5 42.2 %all-reduce.16 = (bf16[1536]{0:T(1024)(128)(2,1)S(1)}, bf16[256]{0:T(256)(128)(2,1)S(1)}, bf16[256]{0:T(256)(128)(2,1)S(1)}, bf16[1536]{0:T(1024)(128)(2,1)S(1)}, bf16[1536]{0:T(1024)(128)(2,1)S(1)}) all-reduce(bf16[1536]{0:T(1024)(128)(2,1)S(1)} %dynamic-update-slice, ...), channel_id=1, replica_groups=mesh['dp'=4,'seq'=8] {'dp','seq'}, use_global_device_ids=true, to_apply=%add | all-reduce | flops 5120 | bytes 20480
  55.1 43.7 %all_gather.62 = bf16[256,1536]{1,0:T(8,128)(2,1)S(1)} all-gather(bf16[8,1536]{1,0:T(8,128)(2,1)} %param.23), channel_id=1, replica_groups=mesh['dp'=4,'seq'=8] {'dp','seq'}, dimensions={0}, use_global_device_ids=true | all-gather | bytes 811008 | tf_op jit(solution)/shard_map/all_gather | solution.py:117
  101.7 41.4 %all_gather.65 = bf16[256,1536]{1,0:T(8,128)(2,1)S(1)} all-gather(bf16[8,1536]{1,0:T(8,128)(2,1)S(1)} %copy-done.51), channel_id=1, replica_groups=mesh['dp'=4,'seq'=8] {'dp','seq'}, dimensions={0}, use_global_device_ids=true | all-gather | bytes 811008 | tf_op jit(solution)/shard_map/all_gather | solution.py:115
  155.0 13.8 all-gather.14.cloned.1.call-done
  171.1 63.2 %all-gather.16.cloned.1.call-done = bf16[1536,1536]{1,0:T(8,128)(2,1)} async-done(((bf16[48,1536]{1,0:T(8,128)(2,1)}), bf16[1536,1536]{1,0:T(8,128)(2,1)}) %all-gather.16.cloned.1.call-update) | async-done | bytes 4718608 | tf_op jit(solution)/shard_map/all_gather | solution.py:113
  257.2 41.9 %all-gather.18.cloned.1.call-done = bf16[1536,1536]{1,0:T(8,128)(2,1)} async-done(((bf16[48,1536]{1,0:T(8,128)(2,1)}), bf16[1536,1536]{1,0:T(8,128)(2,1)}) %all-gather.18.cloned.1.call-update) | async-done | bytes 4718608 | tf_op jit(solution)/shard_map/all_gather | solution.py:119
  303.9 161.8 %all-gather.20.cloned.1.call-done = bf16[8960,1536]{1,0:T(8,128)(2,1)} async-done(((bf16[280,1536]{1,0:T(8,128)(2,1)}), bf16[8960,1536]{1,0:T(8,128)(2,1)}) %all-gather.20.cloned.1.call-update) | async-done | bytes 27525136 | tf_op jit(solution)/shard_map/all_gather | solution.py:165
  465.7 16.7 fusion.50
  482.4 149.8 %all-gather.22.cloned.1.call-done = bf16[8960,1536]{1,0:T(8,128)(2,1)} async-done(((bf16[280,1536]{1,0:T(8,128)(2,1)}), bf16[8960,1536]{1,0:T(8,128)(2,1)}) %all-gather.22.cloned.1.call-update) | async-done | bytes 27525136 | tf_op jit(solution)/shard_map/all_gather | solution.py:166
  632.2 16.4 fusion.51
  648.6 150.2 %all-gather.24.cloned.1.call-done = bf16[1536,8960]{0,1:T(8,128)(2,1)} async-done(((bf16[1536,280]{0,1:T(8,128)(2,1)}), bf16[1536,8960]{0,1:T(8,128)(2,1)}) %all-gather.24.cloned.1.call-update) | async-done | bytes 27525136 | tf_op jit(solution)/shard_map/all_gather | solution.py:167
  798.9 20.1 %multiply_convert_fusion = (bf16[256,8960]{1,0:T(8,128)(2,1)S(1)}, bf16[256,8960]{1,0:T(8,128)(2,1)}, bf16[256,8960]{1,0:T(8,128)(2,1)}) fusion(f32[256,8960]{1,0:T(8,128)} %fusion.50, f32[256,8960]{1,0:T(8,128)} %fusion.51, bf16[256,1536]{1,0:T(8,128)(2,1)S(1)} %copy-done.24, bf16[1536,8960]{0,1:T(8,128)(2,1)} %all-gather.24.cloned.1.call-done), kind=kOutput, calls=%fused_computation | convolution fusion | flops 7083130880 | bytes 60424192 | tf_op jit(solution)/shard_map/dot_general | solution.py:24
  819.0 16.4 fusion.52
  835.4 14.6 multiply_reduce_fusion
  910.6 14.3 all-to-all-done.3
  931.5 28.9 %all-to-all-done = bf16[256,4,384]{0,1,2:T(4,128)(2,1)S(1)} async-done(((bf16[256,4,384]{0,1,2:T(4,128)(2,1)}), bf16[256,4,384]{0,1,2:T(4,128)(2,1)S(1)}, u32[]{:S(2)}, u32[]{:S(2)}) %all-to-all-start) | async-done | bytes 786464 | tf_op jit(solution)/shard_map/all_to_all | solution.py:299
  974.5 6.7 copy.145
  981.2 18.3 %copy.146 = bf16[256,4,2240]{0,1,2:T(4,128)(2,1)} copy(bf16[256,4,2240]{0,2,1:T(8,128)(2,1)} %bitcast.310) | data formatting | bytes 9175040 | tf_op jit(solution)/shard_map/reshape | solution.py:29
  1006.0 57.7 %all-gather.28.cloned.1.call-done = bf16[2048,1536]{0,1:T(8,128)(2,1)} async-done(((bf16[256,1536]{0,1:T(8,128)(2,1)}), bf16[2048,1536]{0,1:T(8,128)(2,1)}) %all-gather.28.cloned.1.call-update) | async-done | bytes 6291472 | tf_op jit(solution)/shard_map/all_gather | solution.py:195
  1076.1 18.2 %copy.150 = bf16[256,4,2240]{0,1,2:T(4,128)(2,1)} copy(bf16[256,4,2240]{0,2,1:T(8,128)(2,1)} %bitcast.311) | data formatting | bytes 9175040 | tf_op jit(solution)/shard_map/reshape | solution.py:29
  1094.3 83.9 %all-to-all-done.4 = bf16[256,4,2240]{0,1,2:T(4,128)(2,1)} async-done(((bf16[256,4,2240]{0,1,2:T(4,128)(2,1)}), bf16[256,4,2240]{0,1,2:T(4,128)(2,1)}, u32[]{:S(2)}, u32[]{:S(2)}) %all-to-all-start.4) | async-done | bytes 4587552 | tf_op jit(solution)/shard_map/all_to_all | solution.py:209
  1202.1 115.5 %all-gather.30.cloned.1.call-done = bf16[2048,1536]{1,0:T(8,128)(2,1)} async-done(((bf16[256,1536]{1,0:T(8,128)(2,1)}), bf16[2048,1536]{1,0:T(8,128)(2,1)}) %all-gather.30.cloned.1.call-update) | async-done | bytes 6291472 | tf_op jit(solution)/shard_map/all_gather | solution.py:196
  1317.6 12.0 convolution_convert_fusion.2
  1336.2 18.2 %copy.154 = bf16[256,4,2240]{0,1,2:T(4,128)(2,1)} copy(bf16[256,4,2240]{0,2,1:T(8,128)(2,1)} %bitcast.315) | data formatting | bytes 9175040 | tf_op jit(solution)/shard_map/reshape | solution.py:29
  1367.8 8.7 convolution_convert_fusion.1
  1376.8 109.0 %all-to-all-done.6 = bf16[256,4,2240]{0,1,2:T(4,128)(2,1)} async-done(((bf16[256,4,2240]{0,1,2:T(4,128)(2,1)}), bf16[256,4,2240]{0,1,2:T(4,128)(2,1)}, u32[]{:S(2)}, u32[]{:S(2)}) %all-to-all-start.6) | async-done | bytes 4587552 | tf_op jit(solution)/shard_map/all_to_all | solution.py:206
  1491.4 12.0 convolution_convert_fusion
  1511.3 14.4 fusion.19
  1536.0 38.2 %all-reduce.15 = (f32[1536]{0:T(1024)S(1)}, f32[1536]{0:T(1024)S(1)}) all-reduce(f32[1536]{0:T(1024)S(1)} %get-tuple-element.16, f32[1536]{0:T(1024)} %get-tuple-element.14), channel_id=4, replica_groups=mesh['dp'=4,'seq'=8] {'dp','seq'}, use_global_device_ids=true, to_apply=%region_13.14.clone | all-reduce | flops 3072 | bytes 24576
  1579.5 10.2 all-reduce.17
  1595.1 37.5 %reduce-scatter.24.cloned.1.call-done = bf16[280,1536]{1,0:T(8,128)(2,1)} async-done(((bf16[1120,1536]{1,0:T(8,128)(2,1)}), bf16[280,1536]{1,0:T(8,128)(2,1)}) %reduce-scatter.24.cloned.1.call-update) | async-done | bytes 860176
  1635.1 46.9 %reduce-scatter.26.cloned.1.call-done = bf16[1536,280]{0,1:T(8,128)(2,1)} async-done(((bf16[1536,1120]{0,1:T(8,128)(2,1)}), bf16[1536,280]{0,1:T(8,128)(2,1)}) %reduce-scatter.26.cloned.1.call-update) | async-done | bytes 860176
  (351 shorter events, 231.5 us)
Async XLA Ops:
  7.2 144.6 %all-gather.12.cloned.1.call-start = ((), (), s32[]{:S(2)}) async-start(), calls=%async_computation.14 | async-start | bytes 1179648 | tf_op jit(solution)/shard_map/all_gather | solution.py:140
  100.5 133.8 %copy-start.9 = (bf16[256,1536]{1,0:T(8,128)(2,1)}, bf16[256,1536]{1,0:T(8,128)(2,1)S(1)}, u32[]{:S(2)}) copy-start(bf16[256,1536]{1,0:T(8,128)(2,1)S(1)} %multiply_convert_fusion.4) | copy-start | bytes 2359300
  101.6 67.3 %all-gather.14.cloned.1.call-start = ((), (), s32[]{:S(2)}) async-start(), calls=%async_computation.15 | async-start | bytes 1179648 | tf_op jit(solution)/shard_map/all_gather | solution.py:139
  146.6 87.7 %all-gather.16.cloned.1.call-start = ((), (), s32[]{:S(2)}) async-start(), calls=%async_computation.16 | async-start | bytes 4866048 | tf_op jit(solution)/shard_map/all_gather | solution.py:113
  147.3 151.8 %all-gather.18.cloned.1.call-start = ((), (), s32[]{:S(2)}) async-start(), calls=%async_computation.17 | async-start | bytes 4866048 | tf_op jit(solution)/shard_map/all_gather | solution.py:119
  147.9 317.8 %all-gather.20.cloned.1.call-start = ((), (), s32[]{:S(2)}) async-start(), calls=%async_computation.18 | async-start | bytes 28385280 | tf_op jit(solution)/shard_map/all_gather | solution.py:165
  148.5 483.7 %all-gather.22.cloned.1.call-start = ((), (), s32[]{:S(2)}) async-start(), calls=%async_computation.19 | async-start | bytes 28385280 | tf_op jit(solution)/shard_map/all_gather | solution.py:166
  149.0 649.8 %all-gather.24.cloned.1.call-start = ((), (), s32[]{:S(2)}) async-start(), calls=%async_computation.20 | async-start | bytes 28385280 | tf_op jit(solution)/shard_map/all_gather | solution.py:167
  149.8 779.0 %reduce-scatter.14.cloned.1.call-start = ((), (), s32[]{:S(2)}) async-start(), calls=%async_computation.21 | async-start | bytes 2359296 | tf_op jit(solution)/shard_map/reduce_scatter | solution.py:273
  303.0 547.1 %copy-start.13 = (f32[256,1536]{1,0:T(8,128)}, f32[256,1536]{1,0:T(8,128)S(1)}, u32[]{:S(2)}) copy-start(f32[256,1536]{1,0:T(8,128)S(1)} %get-tuple-element.58) | copy-start | bytes 4718596
  303.9 328.3 %copy-start.25 = (bf16[256,1536]{1,0:T(8,128)(2,1)}, bf16[256,1536]{1,0:T(8,128)(2,1)S(1)}, u32[]{:S(2)}) copy-start(bf16[256,1536]{1,0:T(8,128)(2,1)S(1)} %multiply_convert_fusion.3) | copy-start | bytes 2359300
  482.4 316.5 %copy-start.24 = (bf16[256,1536]{1,0:T(8,128)(2,1)S(1)}, bf16[256,1536]{1,0:T(8,128)(2,1)}, u32[]{:S(2)}) copy-start(bf16[256,1536]{1,0:T(8,128)(2,1)} %fusion.24) | copy-start | bytes 2359300
  877.8 86.4 %reduce-scatter.16.cloned.1.call-start = ((), (), s32[]{:S(2)}) async-start(), calls=%async_computation.22 | async-start | bytes 2359296 | tf_op jit(solution)/shard_map/reduce_scatter | solution.py:274
  888.1 175.6 %all-gather.28.cloned.1.call-start = ((), (), s32[]{:S(2)}) async-start(), calls=%async_computation.25 | async-start | bytes 7077888 | tf_op jit(solution)/shard_map/all_gather | solution.py:195
  890.3 293.4 %all-gather.26.cloned.1.call-start = ((), (), s32[]{:S(2)}) async-start(), calls=%async_computation.23 | async-start | bytes 7077888 | tf_op jit(solution)/shard_map/all_gather | solution.py:194
  891.1 426.6 %all-gather.30.cloned.1.call-start = ((), (), s32[]{:S(2)}) async-start(), calls=%async_computation.27 | async-start | bytes 7077888 | tf_op jit(solution)/shard_map/all_gather | solution.py:196
  891.6 599.8 %all-gather.32.cloned.1.call-start = ((), (), s32[]{:S(2)}) async-start(), calls=%async_computation.28 | async-start | bytes 7077888 | tf_op jit(solution)/shard_map/all_gather | solution.py:197
  897.7 27.2 %all-to-all-start.3 = ((bf16[256,4,384]{0,1,2:T(4,128)(2,1)}), bf16[256,4,384]{0,1,2:T(4,128)(2,1)}, u32[]{:S(2)}, u32[]{:S(2)}) async-start(bf16[256,4,384]{0,1,2:T(4,128)(2,1)} %copy.142), calls=%async_computation.6 | async-start | bytes 1572864 | tf_op jit(solution)/shard_map/all_to_all | solution.py:296
  924.9 35.5 %all-to-all-start = ((bf16[256,4,384]{0,1,2:T(4,128)(2,1)}), bf16[256,4,384]{0,1,2:T(4,128)(2,1)S(1)}, u32[]{:S(2)}, u32[]{:S(2)}) async-start(bf16[256,4,384]{0,1,2:T(4,128)(2,1)} %copy.133), calls=%async_computation.2 | async-start | bytes 1572864 | tf_op jit(solution)/shard_map/all_to_all | solution.py:299
  960.4 10.5 all-to-all-start.1
  970.9 218.3 %copy-start.34 = (bf16[256,4,64]{0,1,2:T(4,128)(2,1)}, bf16[256,4,64]{0,1,2:T(4,128)(2,1)S(1)}, u32[]{:S(2)}) copy-start(bf16[256,4,64]{0,1,2:T(4,128)(2,1)S(1)} %all-to-all-done.1) | copy-start | bytes 393220
  970.9 28.6 %all-to-all-start.2 = ((bf16[256,4,64]{0,1,2:T(4,128)(2,1)}), bf16[256,4,64]{0,1,2:T(4,128)(2,1)S(1)}, u32[]{:S(2)}, u32[]{:S(2)}) async-start(bf16[256,4,64]{0,1,2:T(4,128)(2,1)} %copy.140), calls=%async_computation.5 | async-start | bytes 262144 | tf_op jit(solution)/shard_map/all_to_all | solution.py:305
  999.5 189.7 %copy-start.36 = (bf16[256,4,64]{0,1,2:T(4,128)(2,1)}, bf16[256,4,64]{0,1,2:T(4,128)(2,1)S(1)}, u32[]{:S(2)}) copy-start(bf16[256,4,64]{0,1,2:T(4,128)(2,1)S(1)} %all-to-all-done.2) | copy-start | bytes 393220
  999.5 178.6 %all-to-all-start.4 = ((bf16[256,4,2240]{0,1,2:T(4,128)(2,1)}), bf16[256,4,2240]{0,1,2:T(4,128)(2,1)}, u32[]{:S(2)}, u32[]{:S(2)}) async-start(bf16[256,4,2240]{0,1,2:T(4,128)(2,1)} %copy.146), calls=%async_computation.8 | async-start | bytes 9175040 | tf_op jit(solution)/shard_map/all_to_all | solution.py:209
  1004.6 522.0 %reduce-scatter.20.cloned.1.call-start = ((), (), s32[]{:S(2)}) async-start(), calls=%async_computation.26 | async-start | bytes 737280 | tf_op jit(solution)/shard_map/reduce_scatter | solution.py:335
  1178.2 180.1 %all-to-all-start.5 = ((bf16[256,4,2240]{0,1,2:T(4,128)(2,1)}), bf16[256,4,2240]{0,1,2:T(4,128)(2,1)}, u32[]{:S(2)}, u32[]{:S(2)}) async-start(bf16[256,4,2240]{0,1,2:T(4,128)(2,1)} %copy.150), calls=%async_computation.9 | async-start | bytes 9175040 | tf_op jit(solution)/shard_map/all_to_all | solution.py:212
  1183.4 344.8 %reduce-scatter.18.cloned.1.call-start = ((), (), s32[]{:S(2)}) async-start(), calls=%async_computation.24 | async-start | bytes 737280 | tf_op jit(solution)/shard_map/reduce_scatter | solution.py:317
  1188.7 402.1 %all-reduce.21.cloned.1.call-start = ((), (), s32[]{:S(2)}) async-start(), calls=%async_computation.32 | async-start | bytes 393216
  1196.5 395.8 %reduce-scatter.22.cloned.1.call-start = ((), (), s32[]{:S(2)}) async-start(), calls=%async_computation.29 | async-start | bytes 4300800
  1358.3 127.5 %all-to-all-start.6 = ((bf16[256,4,2240]{0,1,2:T(4,128)(2,1)}), bf16[256,4,2240]{0,1,2:T(4,128)(2,1)}, u32[]{:S(2)}, u32[]{:S(2)}) async-start(bf16[256,4,2240]{0,1,2:T(4,128)(2,1)} %copy.154), calls=%async_computation.10 | async-start | bytes 9175040 | tf_op jit(solution)/shard_map/all_to_all | solution.py:206
  1362.9 269.6 %reduce-scatter.24.cloned.1.call-start = ((), (), s32[]{:S(2)}) async-start(), calls=%async_computation.30 | async-start | bytes 4300800
  1376.5 305.4 %reduce-scatter.26.cloned.1.call-start = ((), (), s32[]{:S(2)}) async-start(), calls=%async_computation.31 | async-start | bytes 4300800
  (65 other events, 1006.8 us)
Sparse Core Ops, SparseCore 0:
  101.7 21.1 all-gather.11
  146.7 22.1 all-gather.13
  171.9 62.3 all-gather.15
  237.2 61.8 all-gather.17
  302.0 163.6 all-gather.19
  468.6 163.5 all-gather.21
  635.2 163.5 all-gather.23
  877.9 36.6 reduce-scatter.13
  916.9 46.0 reduce-scatter.15
  964.4 99.1 all-gather.27
  1065.3 117.1 all-gather.25
  1184.0 133.5 all-gather.29
  1319.8 102.5 all-gather.31
  1425.1 34.7 reduce-scatter.19
  1462.7 25.4 reduce-scatter.17
  1490.9 42.6 all-reduce.20
  1536.4 46.9 reduce-scatter.21
  1586.3 46.1 reduce-scatter.23
  1635.6 46.3 reduce-scatter.25
where the time goes:
time: 1700 us; the launch traced here: 1690 us
  waiting for transfers between devices  1090 us (64%)
  matrix products  198 us (12%)
  blocking collectives  176 us (10%)
  local copies, waits for them, and re-layouts  137 us (8%)
  other arithmetic  44.1 us (3%)
  starting transfers between devices  31.4 us (2%)
    all_gather x1, waiting for transfers between devices, on_device(): lax.all_gather(gate_weight, ('dp', 'seq'), axis=0, tiled=True)  162 us
    all_gather x1, waiting for transfers between devices, on_device(): lax.all_gather(down_weight, ('dp', 'seq'), axis=1, tiled=True)  150 us
    all_gather x1, waiting for transfers between devices, on_device(): lax.all_gather(up_weight, ('dp', 'seq'), axis=0, tiled=True)  150 us
    all_gather x1, waiting for transfers between devices, on_device(): lax.all_gather(mlp_in, 'seq', axis=0, tiled=True)  115 us
    all_to_all x1, waiting for transfers between devices, on_device(): lax.all_to_all(split_columns(hidden_low, dp_count), 'seq', split_axis=2,...  109 us
    unnamed x3, blocking collectives  90.6 us
    unnamed x23, waiting for transfers between devices  89.4 us
    all_to_all x1, waiting for transfers between devices, on_device(): lax.all_to_all(split_columns(gate_grad, dp_count), 'seq', split_axis=2, c...  83.9 us
  transfers between devices with their start and end apart: 26, of which 16 were waited for; matrix products, arithmetic and copies ran while one was open for 17% of the time, Pallas kernels for 0%

commit v1 on v0

v1 whole, which is shorter than its diff:
```python
import math

import jax
import jax.numpy as jnp
from jax import lax
from jax.sharding import PartitionSpec as P

HEADS = 12
KV_HEADS = 2
HEAD = 128


EPSILON = 1e-06
NEGATIVE = -1e30


def times_transposed(left_side, right_side):
    return lax.dot_general(
        left_side, right_side, (((1,), (1,)), ((), ())), preferred_element_type=jnp.float32
    )


def plain_product(left_side, right_side):
    return jnp.dot(left_side, right_side, preferred_element_type=jnp.float32)


def rope_tables(positions):
    half_size = HEAD // 2
    inverse = jnp.exp(-math.log(1000000.0) * 2.0 * jnp.arange(half_size).astype(jnp.float32) / HEAD)
    angles = positions[:, None] * inverse[None, :]
    angles = jnp.concatenate([angles, angles], axis=1)
    return (jnp.cos(angles), jnp.sin(angles))


def rotate(values, cosine, sine_table):
    half_size = HEAD // 2
    turned = jnp.concatenate([-values[..., half_size:], values[..., :half_size]], axis=-1)
    return values * cosine[:, None, :] + turned * sine_table[:, None, :]


def rotate_back(gradient, cosine, sine_table):
    half_size = HEAD // 2
    scaled = gradient * sine_table[:, None, :]
    turned = jnp.concatenate([scaled[..., half_size:], -scaled[..., :half_size]], axis=-1)
    return gradient * cosine[:, None, :] + turned


def rms_parts(values):
    inverse = lax.rsqrt(jnp.mean(values * values, axis=-1, keepdims=True) + EPSILON)
    return (values * inverse, inverse)


def rms_back(upstream, normal_values, inverse, gain_values):
    scaled = upstream * gain_values
    gain_grad = jnp.sum(upstream * normal_values, axis=0)
    input_part = inverse * (
        scaled - normal_values * jnp.mean(scaled * normal_values, axis=-1, keepdims=True)
    )
    return (input_part, gain_grad)


def masked_scores(query_heads, key_heads, causal, score_scale):
    scores = (
        jnp.einsum("qkgd,skd->kgqs", query_heads, key_heads, preferred_element_type=jnp.float32)
        * score_scale
    )
    return jnp.where(causal[None, None], scores, NEGATIVE)


def weight_grad(columns, inputs_all):
    return lax.dot_general(
        columns, inputs_all, (((0,), (0,)), ((), ())), preferred_element_type=jnp.float32
    ).astype(jnp.bfloat16)


def column_sum(columns):
    return jnp.sum(columns.astype(jnp.float32), axis=0)


ALL = ("dp", "seq")


def swap(values, axis, bit):
    size = lax.axis_size(axis)
    return lax.ppermute(values, axis, [(index, index ^ bit) for index in range(size)])


def gather_dp(block):
    if lax.axis_size("dp") != 4:
        return lax.all_gather(block, "dp", axis=0, tiled=True)
    half = block.shape[1] // 2
    from_x = swap(block, "dp", 1)
    from_y = swap(block, "dp", 2)
    corner = jnp.concatenate(
        [swap(from_x[:, :half], "dp", 2), swap(from_y[:, half:], "dp", 1)], axis=1
    )
    return jnp.concatenate([block, from_x, from_y, corner], axis=0)


def add_low(left_side, right_side):
    total = left_side.astype(jnp.float32) + right_side.astype(jnp.float32)
    return total.astype(jnp.bfloat16)


def scatter_dp(grads):
    if lax.axis_size("dp") != 4:
        return lax.psum_scatter(grads, "dp", scatter_dimension=0, tiled=True).astype(jnp.float32)
    m = grads.shape[0] // 4
    half = grads.shape[1] // 2
    own, to_x, to_y, corner = (grads[i * m : (i + 1) * m] for i in range(4))
    via_x = swap(corner[:, :half], "dp", 1)
    via_y = swap(corner[:, half:], "dp", 2)
    to_y = jnp.concatenate([add_low(to_y[:, :half], via_x), to_y[:, half:]], axis=1)
    to_x = jnp.concatenate([to_x[:, :half], add_low(to_x[:, half:], via_y)], axis=1)
    got_x = swap(to_x, "dp", 1)
    got_y = swap(to_y, "dp", 2)
    return own.astype(jnp.float32) + got_x.astype(jnp.float32) + got_y.astype(jnp.float32)


def pack_rows(pieces, width):
    flat = jnp.concatenate(pieces)
    return jnp.pad(flat, (0, 8 * width - flat.shape[0])).reshape(8, width)


def unpack_rows(rows, sizes):
    flat = rows.reshape(rows.shape[0], -1)
    parts, at = [], 0
    for size in sizes:
        parts.append(flat[:, at : at + size].reshape(-1))
        at += size
    return parts


def gather_seq(block):
    return lax.all_gather(block, "seq", axis=0, tiled=True)


def scatter_seq(parts):
    return lax.psum_scatter(parts, "seq", scatter_dimension=0, tiled=True).astype(jnp.float32)


def on_device(
    hidden_in,
    lengths,
    cotangent,
    attn_gain,
    q_weight,
    q_bias,
    k_weight,
    k_bias,
    v_weight,
    v_bias,
    o_weight,
    mlp_gain,
    gate_weight,
    up_weight,
    down_weight,
):
    micro_count, span_rows, model_width = hidden_in.shape
    rows = micro_count * span_rows
    full_len = span_rows * lax.axis_size("seq")
    shards = lax.axis_size("dp") * lax.axis_size("seq")
    group_share = HEADS // KV_HEADS
    kv_width = KV_HEADS * HEAD
    score_scale = 1.0 / math.sqrt(HEAD)
    positions = lax.axis_index("seq") * span_rows + jnp.arange(span_rows, dtype=jnp.int32)
    cosine, sine_table = rope_tables(positions.astype(jnp.float32))
    causal = positions[:, None] >= jnp.arange(full_len, dtype=jnp.int32)[None, :]
    q_rows, k_rows, units = q_weight.shape[0], k_weight.shape[0], gate_weight.shape[0]
    small_sizes = (q_rows, q_rows, q_rows, k_rows, k_rows)

    small = pack_rows((attn_gain, mlp_gain, q_bias, k_bias, v_bias), model_width)
    attn_block = jnp.concatenate([q_weight, k_weight, v_weight, small], axis=0)
    attn_all = lax.all_gather(attn_block, ALL, axis=0, tiled=False)
    cuts = (0, q_rows, q_rows + k_rows, q_rows + 2 * k_rows)
    query_w = attn_all[:, cuts[0] : cuts[1]].reshape(-1, model_width)
    key_w = attn_all[:, cuts[1] : cuts[2]].reshape(-1, model_width)
    value_w = attn_all[:, cuts[2] : cuts[3]].reshape(-1, model_width)
    gain_one, gain_two, query_b, key_b, value_b = (
        piece.astype(jnp.float32) for piece in unpack_rows(attn_all[:, cuts[3] :], small_sizes)
    )
    output_w = lax.all_gather(o_weight, ALL, axis=0, tiled=True)

    valid_rows = (positions[None, :] < lengths[:, None]).reshape(rows)
    upstream_low = jnp.where(valid_rows[:, None], cotangent.reshape(rows, model_width), 0)
    upstream = upstream_low.astype(jnp.float32)
    upstream_all = gather_seq(upstream_low)
    gate_w, up_w, down_w = (
        gather_dp(gate_weight),
        gather_dp(up_weight),
        gather_dp(down_weight.T),
    )

    inputs = hidden_in.reshape(rows, model_width).astype(jnp.float32)
    normal_one, inverse_one = rms_parts(inputs)
    attn_in = (normal_one * gain_one).astype(jnp.bfloat16)
    query_lin = times_transposed(attn_in, query_w) + query_b
    key_lin = times_transposed(attn_in, key_w) + key_b
    value_lin = times_transposed(attn_in, value_w) + value_b
    query_rot = rotate(
        query_lin.reshape(micro_count, span_rows, HEADS, HEAD), cosine, sine_table
    ).astype(jnp.bfloat16)
    key_rot = (
        rotate(key_lin.reshape(micro_count, span_rows, KV_HEADS, HEAD), cosine, sine_table)
        .astype(jnp.bfloat16)
        .reshape(micro_count, span_rows, kv_width)
    )
    value_low = value_lin.astype(jnp.bfloat16).reshape(micro_count, span_rows, kv_width)
    pair_all = lax.all_gather(
        jnp.concatenate([key_rot, value_low], axis=-1), "seq", axis=1, tiled=True
    )
    key_all, value_all = pair_all[..., :kv_width], pair_all[..., kv_width:]
    query_heads = query_rot.reshape(micro_count, span_rows, KV_HEADS, group_share, HEAD)
    key_heads = key_all.reshape(micro_count, full_len, KV_HEADS, HEAD)
    value_heads = value_all.reshape(micro_count, full_len, KV_HEADS, HEAD)
    mixed_parts = []
    log_parts = []
    for batch_index in range(micro_count):
        scores = masked_scores(
            query_heads[batch_index], key_heads[batch_index], causal, score_scale
        )
        row_top = jnp.max(scores, axis=-1, keepdims=True)
        exponent = jnp.exp(scores - row_top)
        row_total = jnp.sum(exponent, axis=-1, keepdims=True)
        log_parts.append(row_top + jnp.log(row_total))
        soft_low = (exponent / row_total).astype(jnp.bfloat16)
        mixed_heads = jnp.einsum(
            "kgqs,skd->qkgd", soft_low, value_heads[batch_index], preferred_element_type=jnp.float32
        )
        mixed_parts.append(mixed_heads.reshape(span_rows, model_width))
    mixed_low = jnp.concatenate(mixed_parts, axis=0).astype(jnp.bfloat16)
    resid = inputs + times_transposed(mixed_low, output_w)
    normal_two, inverse_two = rms_parts(resid)
    mlp_in = (normal_two * gain_two).astype(jnp.bfloat16)

    mlp_all = gather_seq(mlp_in)
    gate_lin = times_transposed(mlp_all, gate_w)
    up_lin = times_transposed(mlp_all, up_w)
    hidden_grad = times_transposed(upstream_all, down_w)
    gate_sigma = jax.nn.sigmoid(gate_lin)
    hidden_low = (gate_lin * gate_sigma * up_lin).astype(jnp.bfloat16)
    gate_grad = (
        hidden_grad * up_lin * (gate_sigma * (1.0 + gate_lin * (1.0 - gate_sigma)))
    ).astype(jnp.bfloat16)
    up_grad = (hidden_grad * gate_lin * gate_sigma).astype(jnp.bfloat16)
    mlp_part = plain_product(gate_grad, gate_w) + plain_product(up_grad, up_w)
    mlp_in_grad = scatter_seq(mlp_part.astype(jnp.bfloat16))
    result = resid + scatter_seq(plain_product(hidden_low, down_w).astype(jnp.bfloat16))
    block_out = (
        jnp.where(valid_rows[:, None], result, 0.0)
        .astype(jnp.bfloat16)
        .reshape(micro_count, span_rows, model_width)
    )
    gate_w_grad, up_w_grad, down_w_grad = (
        scatter_dp(weight_grad(gate_grad, mlp_all)),
        scatter_dp(weight_grad(up_grad, mlp_all)),
        scatter_dp(weight_grad(hidden_low, upstream_all)).T,
    )

    norm_two_grad, gain_two_grad = rms_back(mlp_in_grad, normal_two, inverse_two, gain_two)
    resid_grad = upstream + norm_two_grad
    resid_low = resid_grad.astype(jnp.bfloat16)
    output_part = weight_grad(resid_low, mixed_low)
    output_w_grad = lax.psum_scatter(output_part, ALL, scatter_dimension=0, tiled=True).astype(
        jnp.float32
    )
    mixed_grad = (
        plain_product(resid_low, output_w)
        .astype(jnp.bfloat16)
        .reshape(micro_count, span_rows, KV_HEADS, group_share, HEAD)
    )
    query_parts = []
    key_parts = []
    value_parts = []
    for batch_index in range(micro_count):
        again_scores = masked_scores(
            query_heads[batch_index], key_heads[batch_index], causal, score_scale
        )
        soft_probs = jnp.exp(again_scores - log_parts[batch_index])
        probs_low = soft_probs.astype(jnp.bfloat16)
        prob_grad = jnp.einsum(
            "qkgd,skd->kgqs",
            mixed_grad[batch_index],
            value_heads[batch_index],
            preferred_element_type=jnp.float32,
        )
        value_all_grad = jnp.einsum(
            "kgqs,qkgd->skd", probs_low, mixed_grad[batch_index], preferred_element_type=jnp.float32
        )
        row_delta = jnp.sum(soft_probs * prob_grad, axis=-1, keepdims=True)
        score_grad = (soft_probs * (prob_grad - row_delta)).astype(jnp.bfloat16)
        query_parts.append(
            jnp.einsum(
                "kgqs,skd->qkgd",
                score_grad,
                key_heads[batch_index],
                preferred_element_type=jnp.float32,
            )
            * score_scale
        )
        key_parts.append(
            (
                jnp.einsum(
                    "kgqs,qkgd->skd",
                    score_grad,
                    query_heads[batch_index],
                    preferred_element_type=jnp.float32,
                )
                * score_scale
            ).reshape(full_len, kv_width)
        )
        value_parts.append(value_all_grad.reshape(full_len, kv_width))
    pair_grad = lax.psum_scatter(
        jnp.concatenate([jnp.stack(key_parts), jnp.stack(value_parts)], axis=-1).astype(
            jnp.bfloat16
        ),
        "seq",
        scatter_dimension=1,
        tiled=True,
    ).astype(jnp.float32)
    key_grad, value_grad = pair_grad[..., :kv_width], pair_grad[..., kv_width:]
    query_grad = jnp.stack(query_parts).reshape(micro_count, span_rows, HEADS, HEAD)
    query_low = (
        rotate_back(query_grad, cosine, sine_table).reshape(rows, model_width).astype(jnp.bfloat16)
    )
    key_low = (
        rotate_back(key_grad.reshape(micro_count, span_rows, KV_HEADS, HEAD), cosine, sine_table)
        .reshape(rows, kv_width)
        .astype(jnp.bfloat16)
    )
    value_grad_low = value_grad.reshape(rows, kv_width).astype(jnp.bfloat16)
    attn_in_grad = (
        plain_product(query_low, query_w)
        + plain_product(key_low, key_w)
        + plain_product(value_grad_low, value_w)
    )
    norm_one_grad, gain_one_grad = rms_back(attn_in_grad, normal_one, inverse_one, gain_one)
    input_grad = (resid_grad + norm_one_grad).reshape(micro_count, span_rows, model_width)
    small_grads = jnp.concatenate(
        [
            piece.reshape(shards, -1)
            for piece in (
                gain_one_grad,
                gain_two_grad,
                column_sum(query_low),
                column_sum(key_low),
                column_sum(value_grad_low),
            )
        ],
        axis=1,
    ).astype(jnp.bfloat16)
    small_grads = jnp.pad(
        small_grads, ((0, 0), (0, 8 * model_width - small_grads.shape[1]))
    ).reshape(shards, 8, model_width)
    grad_block = jnp.concatenate(
        [
            weight_grad(query_low, attn_in).reshape(shards, q_rows, model_width),
            weight_grad(key_low, attn_in).reshape(shards, k_rows, model_width),
            weight_grad(value_grad_low, attn_in).reshape(shards, k_rows, model_width),
            small_grads,
        ],
        axis=1,
    )
    totals = (
        lax.psum_scatter(
            grad_block.reshape(-1, model_width), ALL, scatter_dimension=0, tiled=True
        )
        .astype(jnp.float32)
    )
    small_totals = unpack_rows(totals[None, cuts[3] :], small_sizes)
    return (
        block_out,
        input_grad,
        small_totals[0],
        totals[cuts[0] : cuts[1]],
        small_totals[2],
        totals[cuts[1] : cuts[2]],
        small_totals[3],
        totals[cuts[2] : cuts[3]],
        small_totals[4],
        output_w_grad,
        small_totals[1],
        gate_w_grad,
        up_w_grad,
        down_w_grad,
    )


def solution(mesh):
    placed = (
        P("dp", "seq", None),
        P("dp"),
        P("dp", "seq", None),
        P(("dp", "seq")),
        P(("dp", "seq"), None),
        P(("dp", "seq")),
        P(("dp", "seq"), None),
        P(("dp", "seq")),
        P(("dp", "seq"), None),
        P(("dp", "seq")),
        P(("dp", "seq"), None),
        P(("dp", "seq")),
        P(("dp", "seq"), None),
        P(("dp", "seq"), None),
        P(None, ("dp", "seq")),
    )
    return jax.shard_map(
        on_device,
        mesh=mesh,
        in_specs=placed,
        out_specs=(
            P("dp", "seq", None),
            P("dp", "seq", None),
            P(("dp", "seq")),
            P(("dp", "seq"), None),
            P(("dp", "seq")),
            P(("dp", "seq"), None),
            P(("dp", "seq")),
            P(("dp", "seq"), None),
            P(("dp", "seq")),
            P(("dp", "seq"), None),
            P(("dp", "seq")),
            P(("dp", "seq"), None),
            P(("dp", "seq"), None),
            P(None, ("dp", "seq")),
        ),
        check_vma=False,
    )
```

time: 1700 us -> 871 us (0.51)
  waiting for transfers between devices: 1090 us -> 524 us
  blocking collectives: 176 us -> 0 us
  local copies, waits for them, and re-layouts: 137 us -> 48.6 us
  other arithmetic: 44.1 us -> 63.5 us
    all_gather x11 -> x5, waiting for transfers between devices: 754 us -> 177 us  [the longest x1 72.6 us: on_device(): attn_all = lax.all_gather(attn_block, ALL, axis=0, tiled=False)]
    all_to_all x7 -> x0, waiting for transfers between devices: 245 us -> none  [the longest x1 109 us: on_device(): lax.all_to_all(split_columns(hidden_low, dp_count), 'seq', split_axis=2,...]
    reduce_scatter x4, waiting for transfers between devices: 0.04 us -> 232 us  [the longest x2 123 us: scatter_seq(): lax.psum_scatter(parts, 'seq', scatter_dimension=0, tiled=True)]
    ppermute x0 -> x24, waiting for transfers between devices: none -> 114 us  [swap(): lax.ppermute(values, axis, [(index, index ^ bit) for index in range(size)])]
    unnamed x3 -> x0, blocking collectives: 90.6 us -> none
    unnamed x23 -> x11, waiting for transfers between devices: 89.4 us -> 0.83 us
    all_gather x2 -> x0, blocking collectives: 85.1 us -> none  [the longest x1 43.7 us: on_device(): lax.all_gather(v_weight, ('dp', 'seq'), axis=0, tiled=True)]
    reshape x5 -> x9, local copies, waits for them, and re-layouts: 60 us -> 3.06 us  [the longest x5 1.7 us: on_device(): piece.reshape(shards, -1)]
  transfers between devices with their start and end apart: 26 -> 34, of which waited for: 16 -> 18; matrix products, arithmetic and copies ran while one was open for 17% -> 21% of each run, Pallas kernels for 0% -> 0%
where the time goes in v1:
time: 871 us; the launch traced here: 866 us
  waiting for transfers between devices  524 us (60%)
  matrix products  185 us (21%)
  other arithmetic  63.5 us (7%)
  local copies, waits for them, and re-layouts  48.6 us (6%)
  starting transfers between devices  29.3 us (3%)
  between operations  15.6 us (2%)
    reduce_scatter x2, waiting for transfers between devices, scatter_seq(): lax.psum_scatter(parts, 'seq', scatter_dimension=0, tiled=True)  123 us
    ppermute x24, waiting for transfers between devices, swap(): lax.ppermute(values, axis, [(index, index ^ bit) for index in range(size)])  114 us
    reduce_scatter x1, waiting for transfers between devices, on_device(): lax.psum_scatter(grad_block.reshape(-1, model_width), ALL, scatter_dimens...  109 us
    all_gather x1, waiting for transfers between devices, on_device(): attn_all = lax.all_gather(attn_block, ALL, axis=0, tiled=False)  72.6 us
    dot_general x7, matrix products, times_transposed(): lax.dot_general(left_side, right_side, (((1,), (1,)), ((), ())), preferre...  58.3 us
    all_gather x1, waiting for transfers between devices, on_device(): output_w = lax.all_gather(o_weight, ALL, axis=0, tiled=True)  56 us
    dot_general x7, matrix products, plain_product(): return jnp.dot(left_side, right_side, preferred_element_type=jnp.float32)  54.4 us
    dot_general x7, matrix products, weight_grad(): lax.dot_general(columns, inputs_all, (((0,), (0,)), ((), ())), preferred_...  42.4 us
  transfers between devices with their start and end apart: 34, of which 18 were waited for; matrix products, arithmetic and copies ran while one was open for 21% of the time, Pallas kernels for 0%

profile of v1, /device:TPU:0, one launch (start us, length us, event | category | flops | bytes accessed | tf_op | source)
XLA Modules:
  0.0 865.5 jit_solution(3805706955048203170)
XLA Ops:
  14.8 72.6 %all-gather.15.cloned.1.call-done = bf16[2304,1536]{1,0:T(8,128)(2,1)} async-done(((bf16[72,1536]{1,0:T(8,128)(2,1)}), bf16[2304,1536]{1,0:T(8,128)(2,1)}) %all-gather.15.cloned.1.call-update) | async-done | bytes 7077904 | tf_op jit(solution)/shard_map/all_gather | solution.py:174
  103.2 4.9 convolution_add_fusion.3
  117.8 7.1 all-gather.7.cloned.1.call-done
  134.7 56.0 %all-gather.9.cloned.1.call-done = bf16[1536,1536]{1,0:T(8,128)(2,1)} async-done(((bf16[48,1536]{1,0:T(8,128)(2,1)}), bf16[1536,1536]{1,0:T(8,128)(2,1)}) %all-gather.9.cloned.1.call-update) | async-done | bytes 4718608 | tf_op jit(solution)/shard_map/all_gather | solution.py:182
  202.0 16.7 %collective-permute-done.8 = bf16[280,1536]{1,0:T(8,128)(2,1)S(1)} collective-permute-done((bf16[280,1536]{1,0:T(8,128)(2,1)}, bf16[280,1536]{1,0:T(8,128)(2,1)S(1)}, u32[]{:S(2)}, u32[]{:S(2)}) %collective-permute-start.8) | collective-permute-done | bytes 860192 | tf_op jit(solution)/shard_map/ppermute | solution.py:85
  221.2 16.0 %collective-permute-done.4 = bf16[280,1536]{1,0:T(8,128)(2,1)S(1)} collective-permute-done((bf16[280,1536]{1,0:T(8,128)(2,1)}, bf16[280,1536]{1,0:T(8,128)(2,1)S(1)}, u32[]{:S(2)}, u32[]{:S(2)}) %collective-permute-start.4) | collective-permute-done | bytes 860192 | tf_op jit(solution)/shard_map/ppermute | solution.py:85
  240.2 15.5 %collective-permute-done = bf16[280,1536]{1,0:T(8,128)(2,1)S(1)} collective-permute-done((bf16[280,1536]{1,0:T(8,128)(2,1)}, bf16[280,1536]{1,0:T(8,128)(2,1)S(1)}, u32[]{:S(2)}, u32[]{:S(2)}) %collective-permute-start) | collective-permute-done | bytes 860192 | tf_op jit(solution)/shard_map/ppermute | solution.py:85
  259.2 7.0 collective-permute-done.10
  267.0 12.5 %fusion.71 = f32[2048,1120]{0,1:T(8,128)} fusion(bf16[2048,1536]{1,0:T(8,128)(2,1)} %all-gather.13.cloned.1.call-done, bf16[280,768]{1,0:T(8,128)(2,1)} %collective-permute-done.11, bf16[280,768]{1,0:T(8,128)(2,1)} %copy-done.52, bf16[280,1536]{1,0:T(8,128)(2,1)} %copy-done.37, bf16[280,1536]{1,0:T(8,128)(2,1)} %copy-done.35, bf16[280,1536]{1,0:T(8,128)(2,1)} %bitcast.337), kind=kOutput, calls=%fused_computation.172 | convolution fusion | flops 7063633920 | bytes 18907136 | tf_op jit(solution)/shard_map/dot_general | solution.py:18
  279.6 41.1 %all-gather.11.cloned.1.call-done = bf16[2048,1536]{1,0:T(8,128)(2,1)} async-done(((bf16[256,1536]{1,0:T(8,128)(2,1)}), bf16[2048,1536]{1,0:T(8,128)(2,1)}) %all-gather.11.cloned.1.call-update) | async-done | bytes 6291472 | tf_op jit(solution)/shard_map/all_gather | solution.py:135
  320.7 12.5 %fusion.73 = f32[2048,1120]{0,1:T(8,128)} fusion(bf16[2048,1536]{1,0:T(8,128)(2,1)} %all-gather.11.cloned.1.call-done, bf16[280,768]{1,0:T(8,128)(2,1)} %collective-permute-done.7, bf16[280,768]{1,0:T(8,128)(2,1)} %collective-permute-done.6, bf16[280,1536]{1,0:T(8,128)(2,1)} %copy-done.40, bf16[280,1536]{1,0:T(8,128)(2,1)} %copy-done.38, ...), kind=kOutput, calls=%fused_computation.174 | convolution fusion | flops 7063633920 | bytes 18907136 | tf_op jit(solution)/shard_map/dot_general | solution.py:18
  333.2 21.1 %multiply_convert_fusion.1 = (bf16[2048,1120]{0,1:T(8,128)(2,1)}, bf16[2048,1120]{0,1:T(8,128)(2,1)}, bf16[2048,1120]{0,1:T(8,128)(2,1)}) fusion(f32[2048,1120]{0,1:T(8,128)} %fusion.71, f32[2048,1120]{0,1:T(8,128)} %fusion.73, bf16[2048,1536]{1,0:T(8,128)(2,1)} %all-gather.11.cloned.1.call-done, bf16[280,768]{1,0:T(8,128)(2,1)} %collective-permute-done.3, ...), kind=kOutput, calls=%fused_computation.2 | convolution fusion | flops 7100334080 | bytes 41844736 | tf_op jit(solution)/shard_map/dot_general | solution.py:18
  354.4 14.0 %fusion.72 = f32[2048,1536]{1,0:T(8,128)} fusion(bf16[2048,1120]{0,1:T(8,128)(2,1)} %get-tuple-element.24, bf16[280,768]{1,0:T(8,128)(2,1)} %collective-permute-done.7, bf16[280,768]{1,0:T(8,128)(2,1)} %collective-permute-done.6, bf16[280,1536]{1,0:T(8,128)(2,1)} %copy-done.40, bf16[280,1536]{1,0:T(8,128)(2,1)S(1)} %copy-done.39, bf16[280,1536]{1,0:T(8,128)(2,1)} %param.28), kind=kOutput, calls=%fused_computation.173 | convolution fusion | flops 7063633920 | bytes 20611072 | tf_op jit(solution)/shard_map/dot_general | solution.py:24
  368.4 13.3 %add_convert_fusion = bf16[2048,1536]{1,0:T(8,128)(2,1)} fusion(f32[2048,1536]{1,0:T(8,128)} %fusion.72, bf16[2048,1120]{0,1:T(8,128)(2,1)S(1)} %copy-done.53, bf16[280,768]{1,0:T(8,128)(2,1)} %collective-permute-done.3, bf16[280,768]{1,0:T(8,128)(2,1)} %collective-permute-done.2, bf16[280,1536]{1,0:T(8,128)(2,1)S(1)} %copy-done.44, ...), kind=kOutput, calls=%fused_computation | convolution fusion | flops 7069925376 | bytes 26902528 | tf_op jit(solution)/shard_map/dot_general | solution.py:24
  382.9 12.7 %convolution_convert_fusion = bf16[2048,1536]{1,0:T(8,128)(2,1)} fusion(bf16[2048,1120]{0,1:T(8,128)(2,1)} %get-tuple-element.23, bf16[280,768]{1,0:T(8,128)(2,1)} %collective-permute-done.11, bf16[280,768]{1,0:T(8,128)(2,1)} %copy-done.52, bf16[280,1536]{1,0:T(8,128)(2,1)} %copy-done.37, bf16[280,1536]{1,0:T(8,128)(2,1)S(1)} %copy-done.36, ...), kind=kOutput, calls=%fused_computation.5 | convolution fusion | flops 7066779648 | bytes 14319616 | tf_op jit(solution)/shard_map/dot_general | solution.py:24
  396.1 54.2 %reduce-scatter.10.cloned.1.call-done = bf16[256,1536]{1,0:T(8,128)(2,1)} async-done(((bf16[2048,1536]{1,0:T(8,128)(2,1)}), bf16[256,1536]{1,0:T(8,128)(2,1)}) %reduce-scatter.10.cloned.1.call-update) | async-done | bytes 786448 | tf_op jit(solution)/shard_map/reduce_scatter | solution.py:139
  452.0 68.8 %reduce-scatter.8.cloned.1.call-done = bf16[256,1536]{1,0:T(8,128)(2,1)} async-done(((bf16[2048,1536]{1,0:T(8,128)(2,1)}), bf16[256,1536]{1,0:T(8,128)(2,1)}) %reduce-scatter.8.cloned.1.call-update) | async-done | bytes 786448 | tf_op jit(solution)/shard_map/reduce_scatter | solution.py:139
  529.2 6.6 fusion.3
  535.8 4.9 fusion.43
  542.0 7.2 fusion
  574.6 10.8 %convolution_convert_fusion.1 = bf16[1120,1536]{1,0:T(8,128)(2,1)S(1)} fusion(bf16[2048,1120]{0,1:T(8,128)(2,1)} %get-tuple-element.23, bf16[2048,1536]{1,0:T(8,128)(2,1)} %all-gather.13.cloned.1.call-done), kind=kOutput, calls=%fused_computation.6 | convolution fusion | flops 7048151040 | bytes 14319616 | tf_op jit(solution)/shard_map/dot_general | solution.py:71
  592.8 13.1 %fusion.75 = (bf16[12,128]{1,0:T(8,128)(2,1)S(1)}, bf16[2,128,12,128]{1,0,3,2:T(2,128)(2,1)}) fusion(f32[2,128,12,64]{1,0,3,2:T(2,128)S(1)} %get-tuple-element.48, f32[2,128,12,64]{1,0,3,2:T(2,128)S(1)} %get-tuple-element.47, f32[128,128]{0,1:T(8,128)S(1)} %get-tuple-element.76, f32[1,128,12,128]{1,0,3,2:T(1,128)S(1)} %bitcast.287, ...), kind=kLoop, calls=%fused_computation.176 | loop fusion | flops 2357760 | bytes 4000768 | tf_op jit(solution)/shard_map/reduce_sum | solution.py:77
  606.8 4.8 convolution_convert_fusion.5
  611.6 5.0 fusion.50
  634.4 5.8 pad_maximum_fusion
  640.3 11.0 %convolution_convert_fusion.2 = bf16[1120,1536]{1,0:T(8,128)(2,1)S(1)} fusion(bf16[2048,1120]{0,1:T(8,128)(2,1)} %get-tuple-element.24, bf16[2048,1536]{1,0:T(8,128)(2,1)} %all-gather.11.cloned.1.call-done), kind=kOutput, calls=%fused_computation.7 | convolution fusion | flops 7048151040 | bytes 14319616 | tf_op jit(solution)/shard_map/dot_general | solution.py:71
  654.2 11.4 %convolution_convert_fusion.3 = bf16[1120,1536]{1,0:T(8,128)(2,1)S(1)} fusion(bf16[2048,1120]{0,1:T(8,128)(2,1)} %get-tuple-element.22, bf16[2048,1536]{1,0:T(8,128)(2,1)} %all-gather.11.cloned.1.call-done), kind=kOutput, calls=%fused_computation.8 | convolution fusion | flops 7048151040 | bytes 14319616 | tf_op jit(solution)/shard_map/dot_general | solution.py:71
  673.3 6.8 collective-permute-done.12
  683.4 18.0 %collective-permute-done.21 = bf16[280,1536]{1,0:T(8,128)(2,1)S(1)} collective-permute-done((bf16[280,1536]{1,0:T(8,128)(2,1)S(1)}, bf16[280,1536]{1,0:T(8,128)(2,1)S(1)}, u32[]{:S(2)}, u32[]{:S(2)}) %collective-permute-start.21) | collective-permute-done | bytes 860192 | tf_op jit(solution)/shard_map/ppermute | solution.py:85
  704.2 16.7 %collective-permute-done.17 = bf16[280,1536]{1,0:T(8,128)(2,1)S(1)} collective-permute-done((bf16[280,1536]{1,0:T(8,128)(2,1)S(1)}, bf16[280,1536]{1,0:T(8,128)(2,1)S(1)}, u32[]{:S(2)}, u32[]{:S(2)}) %collective-permute-start.17) | collective-permute-done | bytes 860192 | tf_op jit(solution)/shard_map/ppermute | solution.py:85
  723.7 14.8 %collective-permute-done.13 = bf16[280,1536]{1,0:T(8,128)(2,1)S(1)} collective-permute-done((bf16[280,1536]{1,0:T(8,128)(2,1)S(1)}, bf16[280,1536]{1,0:T(8,128)(2,1)S(1)}, u32[]{:S(2)}, u32[]{:S(2)}) %collective-permute-start.13) | collective-permute-done | bytes 860192 | tf_op jit(solution)/shard_map/ppermute | solution.py:85
  744.1 109.0 %reduce-scatter.12.cloned.1.call-done = bf16[72,1536]{1,0:T(8,128)(2,1)} async-done(((bf16[2304,1536]{1,0:T(8,128)(2,1)}), bf16[72,1536]{1,0:T(8,128)(2,1)}) %reduce-scatter.12.cloned.1.call-update) | async-done | bytes 221200 | tf_op jit(solution)/shard_map/reduce_scatter | solution.py:365
  (312 shorter events, 157.8 us)
Async XLA Ops:
  7.2 80.2 %all-gather.15.cloned.1.call-start = ((), (), s32[]{:S(2)}) async-start(), calls=%async_computation.13 | async-start | bytes 7299072 | tf_op jit(solution)/shard_map/all_gather | solution.py:174
  12.5 112.4 %all-gather.7.cloned.1.call-start = ((), (), s32[]{:S(2)}) async-start(), calls=%async_computation.5 | async-start | bytes 2359296 | tf_op jit(solution)/shard_map/all_gather | solution.py:209
  95.6 95.1 %all-gather.9.cloned.1.call-start = ((), (), s32[]{:S(2)}) async-start(), calls=%async_computation.6 | async-start | bytes 4866048 | tf_op jit(solution)/shard_map/all_gather | solution.py:182
  96.3 170.7 %all-gather.13.cloned.1.call-start = ((), (), s32[]{:S(2)}) async-start(), calls=%async_computation.9 | async-start | bytes 7077888 | tf_op jit(solution)/shard_map/all_gather | solution.py:135
  98.2 222.5 %all-gather.11.cloned.1.call-start = ((), (), s32[]{:S(2)}) async-start(), calls=%async_computation.7 | async-start | bytes 7077888 | tf_op jit(solution)/shard_map/all_gather | solution.py:135
  195.9 254.4 %reduce-scatter.10.cloned.1.call-start = ((), (), s32[]{:S(2)}) async-start(), calls=%async_computation.10 | async-start | bytes 7077888 | tf_op jit(solution)/shard_map/reduce_scatter | solution.py:139
  196.5 22.3 %collective-permute-start.8 = (bf16[280,1536]{1,0:T(8,128)(2,1)}, bf16[280,1536]{1,0:T(8,128)(2,1)S(1)}, u32[]{:S(2)}, u32[]{:S(2)}) collective-permute-start(bf16[280,1536]{1,0:T(8,128)(2,1)} %bitcast.335), channel_id=1, source_target_pairs={{0,8},{8,0},{16,24},{24,16},{1,9},{9,1},{17,25},{25,17},{2,10},{10... | collective-permute-start | bytes 2580488 | tf_op jit(solution)/shard_map/ppermute | solution.py:85
  198.0 22.3 %collective-permute-start.9 = (bf16[280,1536]{1,0:T(8,128)(2,1)}, bf16[280,1536]{1,0:T(8,128)(2,1)S(1)}, u32[]{:S(2)}, u32[]{:S(2)}) collective-permute-start(bf16[280,1536]{1,0:T(8,128)(2,1)} %bitcast.336), channel_id=1, source_target_pairs={{0,16},{8,24},{16,0},{24,8},{1,17},{9,25},{17,1},{25,9},{2,18},{10... | collective-permute-start | bytes 2580488 | tf_op jit(solution)/shard_map/ppermute | solution.py:85
  198.6 38.6 %collective-permute-start.4 = (bf16[280,1536]{1,0:T(8,128)(2,1)}, bf16[280,1536]{1,0:T(8,128)(2,1)S(1)}, u32[]{:S(2)}, u32[]{:S(2)}) collective-permute-start(bf16[280,1536]{1,0:T(8,128)(2,1)} %param.28), channel_id=1, source_target_pairs={{0,8},{8,0},{16,24},{24,16},{1,9},{9,1},{17,25},{25,17},{2,10},{10... | collective-permute-start | bytes 2580488 | tf_op jit(solution)/shard_map/ppermute | solution.py:85
  200.1 38.6 %collective-permute-start.5 = (bf16[280,1536]{1,0:T(8,128)(2,1)}, bf16[280,1536]{1,0:T(8,128)(2,1)S(1)}, u32[]{:S(2)}, u32[]{:S(2)}) collective-permute-start(bf16[280,1536]{1,0:T(8,128)(2,1)} %param.28), channel_id=1, source_target_pairs={{0,16},{8,24},{16,0},{24,8},{1,17},{9,25},{17,1},{25,9},{2,18},{10... | collective-permute-start | bytes 2580488 | tf_op jit(solution)/shard_map/ppermute | solution.py:85
  200.6 55.0 %collective-permute-start = (bf16[280,1536]{1,0:T(8,128)(2,1)}, bf16[280,1536]{1,0:T(8,128)(2,1)S(1)}, u32[]{:S(2)}, u32[]{:S(2)}) collective-permute-start(bf16[280,1536]{1,0:T(8,128)(2,1)} %param.27), channel_id=1, source_target_pairs={{0,8},{8,0},{16,24},{24,16},{1,9},{9,1},{17,25},{25,17},{2,10},{10... | collective-permute-start | bytes 2580488 | tf_op jit(solution)/shard_map/ppermute | solution.py:85
  218.8 39.1 %collective-permute-start.1 = (bf16[280,1536]{1,0:T(8,128)(2,1)}, bf16[280,1536]{1,0:T(8,128)(2,1)S(1)}, u32[]{:S(2)}, u32[]{:S(2)}) collective-permute-start(bf16[280,1536]{1,0:T(8,128)(2,1)} %param.27), channel_id=1, source_target_pairs={{0,16},{8,24},{16,0},{24,8},{1,17},{9,25},{17,1},{25,9},{2,18},{10... | collective-permute-start | bytes 2580488 | tf_op jit(solution)/shard_map/ppermute | solution.py:85
  220.3 46.0 %collective-permute-start.10 = (bf16[280,768]{1,0:T(8,128)(2,1)S(1)}, bf16[280,768]{1,0:T(8,128)(2,1)S(1)}, u32[]{:S(2)}, u32[]{:S(2)}) collective-permute-start(bf16[280,768]{1,0:T(8,128)(2,1)S(1)} %slice.333), channel_id=1, source_target_pairs={{0,16},{8,24},{16,0},{24,8},{1,17},{9,25},{17,1},{25,9},{2,18},{10... | collective-permute-start | bytes 1290248 | tf_op jit(solution)/shard_map/ppermute | solution.py:85
  237.2 29.8 %collective-permute-start.11 = (bf16[280,768]{1,0:T(8,128)(2,1)S(1)}, bf16[280,768]{1,0:T(8,128)(2,1)}, u32[]{:S(2)}, u32[]{:S(2)}) collective-permute-start(bf16[280,768]{1,0:T(8,128)(2,1)S(1)} %slice.334), channel_id=1, source_target_pairs={{0,8},{8,0},{16,24},{24,16},{1,9},{9,1},{17,25},{25,17},{2,10},{10... | collective-permute-start | bytes 1290248 | tf_op jit(solution)/shard_map/ppermute | solution.py:85
  238.7 40.9 %collective-permute-start.6 = (bf16[280,768]{1,0:T(8,128)(2,1)S(1)}, bf16[280,768]{1,0:T(8,128)(2,1)}, u32[]{:S(2)}, u32[]{:S(2)}) collective-permute-start(bf16[280,768]{1,0:T(8,128)(2,1)S(1)} %slice.331), channel_id=1, source_target_pairs={{0,16},{8,24},{16,0},{24,8},{1,17},{9,25},{17,1},{25,9},{2,18},{10... | collective-permute-start | bytes 1290248 | tf_op jit(solution)/shard_map/ppermute | solution.py:85
  255.6 23.9 %collective-permute-start.7 = (bf16[280,768]{1,0:T(8,128)(2,1)}, bf16[280,768]{1,0:T(8,128)(2,1)}, u32[]{:S(2)}, u32[]{:S(2)}) collective-permute-start(bf16[280,768]{1,0:T(8,128)(2,1)} %slice.332), channel_id=1, source_target_pairs={{0,8},{8,0},{16,24},{24,16},{1,9},{9,1},{17,25},{25,17},{2,10},{10... | collective-permute-start | bytes 1290248 | tf_op jit(solution)/shard_map/ppermute | solution.py:85
  257.9 75.3 %collective-permute-start.2 = (bf16[280,768]{1,0:T(8,128)(2,1)}, bf16[280,768]{1,0:T(8,128)(2,1)}, u32[]{:S(2)}, u32[]{:S(2)}) collective-permute-start(bf16[280,768]{1,0:T(8,128)(2,1)} %slice.329), channel_id=1, source_target_pairs={{0,16},{8,24},{16,0},{24,8},{1,17},{9,25},{17,1},{25,9},{2,18},{10... | collective-permute-start | bytes 1290248 | tf_op jit(solution)/shard_map/ppermute | solution.py:85
  266.3 66.9 %collective-permute-start.3 = (bf16[280,768]{1,0:T(8,128)(2,1)}, bf16[280,768]{1,0:T(8,128)(2,1)}, u32[]{:S(2)}, u32[]{:S(2)}) collective-permute-start(bf16[280,768]{1,0:T(8,128)(2,1)} %slice.330), channel_id=1, source_target_pairs={{0,8},{8,0},{16,24},{24,16},{1,9},{9,1},{17,25},{25,17},{2,10},{10... | collective-permute-start | bytes 1290248 | tf_op jit(solution)/shard_map/ppermute | solution.py:85
  381.8 139.0 %reduce-scatter.8.cloned.1.call-start = ((), (), s32[]{:S(2)}) async-start(), calls=%async_computation.8 | async-start | bytes 7077888 | tf_op jit(solution)/shard_map/reduce_scatter | solution.py:139
  395.6 221.0 %reduce-scatter.16.cloned.1.call-start = ((), (), s32[]{:S(2)}) async-start(), calls=%async_computation.14 | async-start | bytes 2359296
  569.5 173.0 %reduce-scatter.14.cloned.1.call-start = ((), (), s32[]{:S(2)}) async-start(), calls=%async_computation.12 | async-start | bytes 4866048 | tf_op jit(solution)/shard_map/reduce_scatter | solution.py:264
  574.6 278.6 %reduce-scatter.12.cloned.1.call-start = ((), (), s32[]{:S(2)}) async-start(), calls=%async_computation.11 | async-start | bytes 7299072 | tf_op jit(solution)/shard_map/reduce_scatter | solution.py:365
  586.7 79.3 %collective-permute-start.20 = (bf16[280,768]{1,0:T(8,128)(2,1)}, bf16[280,768]{1,0:T(8,128)(2,1)}, u32[]{:S(2)}, u32[]{:S(2)}) collective-permute-start(bf16[280,768]{1,0:T(8,128)(2,1)} %get-tuple-element.28), channel_id=1, source_target_pairs={{0,16},{8,24},{16,0},{24,8},{1,17},{9,25},{17,1},{25,9},{2,18},{10... | collective-permute-start | bytes 1290248 | tf_op jit(solution)/shard_map/ppermute | solution.py:85
  588.2 78.6 %collective-permute-start.22 = (bf16[280,768]{1,0:T(8,128)(2,1)}, bf16[280,768]{1,0:T(8,128)(2,1)}, u32[]{:S(2)}, u32[]{:S(2)}) collective-permute-start(bf16[280,768]{1,0:T(8,128)(2,1)} %get-tuple-element.27), channel_id=1, source_target_pairs={{0,8},{8,0},{16,24},{24,16},{1,9},{9,1},{17,25},{25,17},{2,10},{10... | collective-permute-start | bytes 1290248 | tf_op jit(solution)/shard_map/ppermute | solution.py:85
  651.3 18.3 %collective-permute-start.16 = (bf16[280,768]{1,0:T(8,128)(2,1)S(1)}, bf16[280,768]{1,0:T(8,128)(2,1)S(1)}, u32[]{:S(2)}, u32[]{:S(2)}) collective-permute-start(bf16[280,768]{1,0:T(8,128)(2,1)S(1)} %get-tuple-element.34), channel_id=1, source_target_pairs={{0,16},{8,24},{16,0},{24,8},{1,17},{9,25},{17,1},{25,9},{2,18},{10... | collective-permute-start | bytes 1290248 | tf_op jit(solution)/shard_map/ppermute | solution.py:85
  652.7 18.9 %collective-permute-start.18 = (bf16[280,768]{1,0:T(8,128)(2,1)S(1)}, bf16[280,768]{1,0:T(8,128)(2,1)S(1)}, u32[]{:S(2)}, u32[]{:S(2)}) collective-permute-start(bf16[280,768]{1,0:T(8,128)(2,1)S(1)} %get-tuple-element.33), channel_id=1, source_target_pairs={{0,8},{8,0},{16,24},{24,16},{1,9},{9,1},{17,25},{25,17},{2,10},{10... | collective-permute-start | bytes 1290248 | tf_op jit(solution)/shard_map/ppermute | solution.py:85
  668.2 33.2 %collective-permute-start.21 = (bf16[280,1536]{1,0:T(8,128)(2,1)S(1)}, bf16[280,1536]{1,0:T(8,128)(2,1)S(1)}, u32[]{:S(2)}, u32[]{:S(2)}) collective-permute-start(bf16[280,1536]{1,0:T(8,128)(2,1)S(1)} %pad_maximum_fusion.6), channel_id=1, source_target_pairs={{0,8},{8,0},{16,24},{24,16},{1,9},{9,1},{17,25},{25,17},{2,10},{10... | collective-permute-start | bytes 2580488 | tf_op jit(solution)/shard_map/ppermute | solution.py:85
  669.6 33.1 %collective-permute-start.23 = (bf16[280,1536]{1,0:T(8,128)(2,1)S(1)}, bf16[280,1536]{1,0:T(8,128)(2,1)S(1)}, u32[]{:S(2)}, u32[]{:S(2)}) collective-permute-start(bf16[280,1536]{1,0:T(8,128)(2,1)S(1)} %pad_maximum_fusion.7), channel_id=1, source_target_pairs={{0,16},{8,24},{16,0},{24,8},{1,17},{9,25},{17,1},{25,9},{2,18},{10... | collective-permute-start | bytes 2580488 | tf_op jit(solution)/shard_map/ppermute | solution.py:85
  671.9 49.1 %collective-permute-start.17 = (bf16[280,1536]{1,0:T(8,128)(2,1)S(1)}, bf16[280,1536]{1,0:T(8,128)(2,1)S(1)}, u32[]{:S(2)}, u32[]{:S(2)}) collective-permute-start(bf16[280,1536]{1,0:T(8,128)(2,1)S(1)} %pad_maximum_fusion.4), channel_id=1, source_target_pairs={{0,8},{8,0},{16,24},{24,16},{1,9},{9,1},{17,25},{25,17},{2,10},{10... | collective-permute-start | bytes 2580488 | tf_op jit(solution)/shard_map/ppermute | solution.py:85
  680.1 42.1 %collective-permute-start.19 = (bf16[280,1536]{1,0:T(8,128)(2,1)S(1)}, bf16[280,1536]{1,0:T(8,128)(2,1)S(1)}, u32[]{:S(2)}, u32[]{:S(2)}) collective-permute-start(bf16[280,1536]{1,0:T(8,128)(2,1)S(1)} %pad_maximum_fusion.5), channel_id=1, source_target_pairs={{0,16},{8,24},{16,0},{24,8},{1,17},{9,25},{17,1},{25,9},{2,18},{10... | collective-permute-start | bytes 2580488 | tf_op jit(solution)/shard_map/ppermute | solution.py:85
  681.4 57.0 %collective-permute-start.13 = (bf16[280,1536]{1,0:T(8,128)(2,1)S(1)}, bf16[280,1536]{1,0:T(8,128)(2,1)S(1)}, u32[]{:S(2)}, u32[]{:S(2)}) collective-permute-start(bf16[280,1536]{1,0:T(8,128)(2,1)S(1)} %pad_maximum_fusion.2), channel_id=1, source_target_pairs={{0,8},{8,0},{16,24},{24,16},{1,9},{9,1},{17,25},{25,17},{2,10},{10... | collective-permute-start | bytes 2580488 | tf_op jit(solution)/shard_map/ppermute | solution.py:85
  701.5 37.9 %collective-permute-start.15 = (bf16[280,1536]{1,0:T(8,128)(2,1)S(1)}, bf16[280,1536]{1,0:T(8,128)(2,1)S(1)}, u32[]{:S(2)}, u32[]{:S(2)}) collective-permute-start(bf16[280,1536]{1,0:T(8,128)(2,1)S(1)} %pad_maximum_fusion.3), channel_id=1, source_target_pairs={{0,16},{8,24},{16,0},{24,8},{1,17},{9,25},{17,1},{25,9},{2,18},{10... | collective-permute-start | bytes 2580488 | tf_op jit(solution)/shard_map/ppermute | solution.py:85
  (60 other events, 723.0 us)
Sparse Core Ops, SparseCore 0:
  12.6 74.7 all-gather.14
  95.7 29.1 all-gather.6
  127.9 62.7 all-gather.8
  192.8 62.9 all-gather.12
  257.3 63.3 all-gather.10
  381.9 68.3 reduce-scatter.9
  452.6 68.1 reduce-scatter.7
  569.6 34.3 reduce-scatter.15
  609.5 119.4 reduce-scatter.13
  734.5 118.5 reduce-scatter.11
